TPU v7x, 128 devices: a whole 4x4x4 slice. The times are simulated.
128 devices in a mesh: ctx: 16 (over x, y), head: 8 (over z, core).
Axes of the slice: x: 4, y: 4, z: 4, core: 2. Of those that a mesh axis runs over, the one named last changes fastest.
Arguments:
- queries: bfloat16 [4, 6144, 6144], P(None, 'ctx', 'head'), may hold values from -6 to 6
- keys_values: bfloat16 [4, 6144, 3072], P(None, 'ctx', 'head'), may hold values from -25 to 25
- block_lists: int32 [4, 48, 16], P(None, 'ctx'), may hold values from -1 to 47, as said below
- starts: int32 [4], replicated, may hold values from 0 to 3071, as said below
- norm_gain: bfloat16 [6144], P('head'), may hold values from 0.5 to 1.5
Outputs:
- mixed_out: bfloat16 [4, 6144, 6144], P(None, 'ctx', 'head')
Inputs may be any that keep to these rules, and one draw needn't show every extreme that they name: `block_lists`: entry [b, j, s] is a block of 128 positions of prompt b, or -1 for an unused slot. The entries of one list are distinct blocks from the prompt's first block (the block holding starts[b]) up to j, always including that first block and j itself; a list is all -1 where j lies before the first block. For each prompt, the lists of the query blocks held by one index of ctx name at most one block held by any other index of ctx, and this bound is reached. One prompt starts at 0 and one at 3071.
All inputs are finite; a program needn't handle non-finite values.
Results may differ from a plain program's by a relative error of at most 0.0041.
Values may be sent and summed in bfloat16 or wider, within the bound.
A program may use at most 128 MiB of HBM per device.

v0:
```python
import math
import jax
import jax.numpy as jnp
from jax import lax
from jax.sharding import PartitionSpec as P

HD = 96
BLK = 128
TOPK = 16
epsilon = 1e-06
masked_score = -1e30


def prefix(shard, axis, combine, identity):
    count, mine = (lax.axis_size(axis), lax.axis_index(axis))
    everything = jax.tree.map(
        lambda part, kind: lax.all_gather(part.astype(kind), axis),
        shard,
        (jnp.bfloat16, jnp.bfloat16),
    )
    start = jax.tree.map(
        lambda part, zero: jnp.broadcast_to(jnp.asarray(zero, part.dtype), part.shape),
        shard,
        identity,
    )

    def step(k, before):
        reached = k < mine
        new = combine(
            before, jax.tree.map(lambda part, own: part[k].astype(own.dtype), everything, shard)
        )
        return jax.tree.map(lambda a, b: jnp.where(reached, a, b), new, before)

    return lax.fori_loop(0, count, step, start)


def feature_map(values):
    return jax.nn.elu(values) + 1.0


def add_states(earlier, later):
    return (earlier[0] + later[0], earlier[1] + later[1])


def on_device(queries, keys_values, block_lists, starts, norm_gain):
    seq_count, local_len, feature_count = queries.shape
    kv_width = keys_values.shape[2]
    kv_local = kv_width // (2 * HD)
    group_size = feature_count // HD // kv_local
    stretch_count = local_len // BLK
    ctx_rank = lax.axis_index("ctx")
    highest = lax.Precision.HIGHEST
    positions = ctx_rank * local_len + jnp.arange(local_len, dtype=jnp.int32)
    usable = positions[None, :] >= starts[:, None]
    usable_stretches = usable.reshape(seq_count, stretch_count, BLK)
    query_stretches = queries.reshape(seq_count, stretch_count, BLK, kv_local, group_size, HD)
    kv_stretches = keys_values.reshape(seq_count, stretch_count, BLK, kv_local, 2, HD)
    value_stretches = kv_stretches[:, :, :, :, 1, :]
    phi_query = lax.optimization_barrier(
        feature_map(query_stretches.astype(jnp.float32)).astype(jnp.bfloat16)
    )
    phi_key = (
        feature_map(kv_stretches[:, :, :, :, 0, :].astype(jnp.float32))
        * usable_stretches[:, :, :, None, None]
    ).astype(jnp.bfloat16)
    stretch_states = jnp.einsum(
        "bctgd,bctge->bcgde", phi_key, value_stretches, preferred_element_type=jnp.float32
    )
    stretch_normals = jnp.sum(phi_key.astype(jnp.float32), axis=2)
    device_state = jnp.sum(stretch_states, axis=1)
    device_normal = jnp.sum(stretch_normals, axis=1)
    identity = (jnp.zeros_like(device_state), jnp.zeros_like(device_normal))
    prior_state, prior_normal = prefix((device_state, device_normal), "ctx", add_states, identity)
    running_state = prior_state[:, None] + jnp.cumsum(stretch_states, axis=1) - stretch_states
    running_normal = prior_normal[:, None] + jnp.cumsum(stretch_normals, axis=1) - stretch_normals
    causal = jnp.arange(BLK)[:, None] >= jnp.arange(BLK)[None, :]
    inner_scores = jnp.einsum(
        "bctgxd,bcsgd->bcgxts", phi_query, phi_key, preferred_element_type=jnp.float32
    )
    inner_scores = jnp.where(causal, inner_scores, 0.0)
    inner_sum = jnp.transpose(jnp.sum(inner_scores, axis=-1), (0, 1, 4, 2, 3))
    inner_num = jnp.einsum(
        "bcgxts,bcsge->bctgxe",
        inner_scores.astype(jnp.bfloat16),
        value_stretches,
        preferred_element_type=jnp.float32,
    )
    query_float = phi_query.astype(jnp.float32)
    state_num = jnp.einsum("bctgxd,bcgde->bctgxe", query_float, running_state, precision=highest)
    state_den = jnp.einsum("bctgxd,bcgd->bctgx", query_float, running_normal, precision=highest)
    row_usable = usable_stretches[:, :, :, None, None]
    denominator = jnp.where(row_usable, inner_sum + state_den, 1.0)
    linear_out = jnp.where(
        row_usable[..., None], (inner_num + state_num) / denominator[..., None], 0.0
    )
    linear_out = linear_out.reshape(seq_count, local_len, feature_count)
    kv_blocks = keys_values.reshape(seq_count, stretch_count, BLK, kv_width)
    candidates = lax.all_gather(kv_blocks, "ctx", axis=1, tiled=True)
    slot_ids = jnp.maximum(block_lists, 0)
    offsets = jnp.arange(BLK, dtype=jnp.int32)
    score_scale = 1.0 / math.sqrt(HD)
    query_rows = positions.reshape(stretch_count, BLK)

    def attend(number):
        seq_index = number // stretch_count
        stretch_index = number % stretch_count
        query_block = lax.dynamic_index_in_dim(
            lax.dynamic_index_in_dim(query_stretches, seq_index, 0, False), stretch_index, 0, False
        )
        seq_pool = lax.dynamic_index_in_dim(candidates, seq_index, 0, False)
        chosen = lax.dynamic_index_in_dim(
            lax.dynamic_index_in_dim(block_lists, seq_index, 0, False), stretch_index, 0, False
        )
        block_slots = lax.dynamic_index_in_dim(
            lax.dynamic_index_in_dim(slot_ids, seq_index, 0, False), stretch_index, 0, False
        )
        picked = jnp.take(seq_pool, block_slots, axis=0).reshape(TOPK * BLK, kv_local, 2, HD)
        key_pos = (jnp.maximum(chosen, 0)[:, None] * BLK + offsets[None, :]).reshape(TOPK * BLK)
        listed = jnp.repeat(chosen >= 0, BLK)
        query_pos = lax.dynamic_index_in_dim(query_rows, stretch_index, 0, False)
        first_live = lax.dynamic_index_in_dim(starts, seq_index, 0, False)
        allowed = (
            listed[None, :]
            & (key_pos[None, :] <= query_pos[:, None])
            & (key_pos[None, :] >= first_live)
        )
        scores = (
            jnp.einsum(
                "xghd,kgd->ghxk",
                query_block,
                picked[:, :, 0, :],
                preferred_element_type=jnp.float32,
            )
            * score_scale
        )
        scores = jnp.where(allowed[None, None], scores, masked_score)
        top_score = jnp.max(scores, axis=-1, keepdims=True)
        weights = jnp.where(allowed[None, None], jnp.exp(scores - top_score), 0.0)
        weight_sum = jnp.transpose(jnp.sum(weights, axis=-1), (2, 0, 1))
        gathered = jnp.einsum(
            "ghxk,kge->xghe",
            weights.astype(jnp.bfloat16),
            picked[:, :, 1, :],
            preferred_element_type=jnp.float32,
        )
        row_ok = (query_pos >= first_live)[:, None, None]
        result = jnp.where(
            row_ok[..., None], gathered / jnp.where(row_ok, weight_sum, 1.0)[..., None], 0.0
        )
        return result.reshape(BLK, feature_count)

    sparse_parts = lax.map(attend, jnp.arange(seq_count * stretch_count, dtype=jnp.int32))
    sparse_out = sparse_parts.reshape(seq_count, local_len, feature_count)
    combined = linear_out + sparse_out
    squares = jnp.sum(combined * combined, axis=-1)
    all_squares = lax.psum(squares, "head")
    full_width = feature_count * lax.axis_size("head")
    scaled = (
        combined
        * lax.rsqrt(all_squares / full_width + epsilon)[..., None]
        * norm_gain.astype(jnp.float32)
    )
    return scaled.astype(jnp.bfloat16)


def solution(mesh):
    return jax.shard_map(
        on_device,
        mesh=mesh,
        in_specs=(
            P(None, "ctx", "head"),
            P(None, "ctx", "head"),
            P(None, "ctx", None),
            P(),
            P("head"),
        ),
        out_specs=P(None, "ctx", "head"),
        check_vma=False,
    )
```

profile of v0, /device:TPU:0, one launch (start us, length us, event | category | flops | bytes accessed | tf_op | source)
XLA Modules:
  0.0 765.6 jit_solution(8744335096811571887)
XLA Ops:
  23.0 6.5 reshape.308
  38.3 23.7 %all-gather.1 = bf16[64,2,96]{2,1,0:T(2,128)(2,1)S(1)} all-gather(bf16[4,2,96]{2,1,0:T(2,128)(2,1)S(1)} %fusion.66), channel_id=3, replica_groups=mesh['ctx'=16,'head'=8] {'ctx'}, dimensions={0}, use_global_device_ids=true | all-gather | bytes 26112 | tf_op jit(solution)/shard_map/all_gather | solution.py:17
  72.7 19.1 %while.31 = (s32[]{:T(128)}, f32[4,2,96,96]{3,2,1,0:T(8,128)S(1)}, f32[4,2,96]{2,1,0:T(2,128)S(1)}, s32[]{:T(128)}, bf16[16,4,2,96,96]{4,3,2,1,0:T(8,128)(2,1)},...) while((s32[]{:T(128)}, f32[4,2,96,96]{3,2,1,0:T(8,128)S(1)}, ...), condition=%wide.region_3.4_spmd.clone, body=%wide.region_2.3_spmd.clone.sunk | while | flops 297988 | bytes 745083 | solution.py:34
  93.8 101.9 %all-gather.5.cloned.1.call-done = bf16[4,48,128,384]{3,2,1,0:T(8,128)(2,1)} async-done(((bf16[4,3,128,384]{3,2,1,0:T(8,128)(2,1)}), bf16[4,48,128,384]{3,2,1,0:T(8,128)(2,1)}) %all-gather.5.cloned.1.call-update) | async-done | bytes 18874384 | tf_op jit(solution)/shard_map/all_gather | solution.py:98
  196.3 511.6 %while.30 = (s32[]{:T(128)}, f32[12,128,768]{1,2,0:T(8,128)}, s32[12]{0:T(128)}, s32[3,128]{1,0:T(4,128)S(1)}, s32[4]{0:T(128)S(1)}, /*index=5*/s32[4,3,16]{2,1,...) while((s32[]{:T(128)}, f32[12,128,768]{1,2,0:T(8,128)}, ...), condition=%wide.region_11.12_spmd.clone, body=%wide.region_8.11_spmd.clone.sunk | while | flops 819669376 | bytes 34196880 | solution.py:152
  214.9 6.3 reshape.344
  228.0 7.2 fusion.98
  257.6 6.3 reshape.344
  270.7 7.2 fusion.98
  313.4 7.2 fusion.98
  356.0 7.2 fusion.98
  385.6 6.3 reshape.344
  398.7 7.2 fusion.98
  441.3 7.2 fusion.98
  484.1 7.2 fusion.98
  526.8 7.2 fusion.98
  569.5 7.2 fusion.98
  611.9 7.2 fusion.98
  654.4 7.2 fusion.98
  696.8 7.2 fusion.98
  714.1 8.8 %multiply_reduce_fusion = (f32[4,3,128]{2,1,0:T(4,128)S(1)}, f32[4,3,128,2,4,96]{2,5,4,3,1,0:T(8,128)}) fusion(f32[4,3,128,2,4,96]{2,5,4,3,1,0:T(8,128)} %bitcast.223, f32[4,3,128,2,4]{2,4,3,1,0:T(4,128)} %fusion.64, f32[4,3,2,96,96,1]{4,3,5,2,1,0:T(8,128)S(1)} %fusion.53, bf16[4,3,128,2,4,96]{2,5,4,3,1,0:T(8,128)(2,1)S(1)} %copy-done.1, ...), kind=kOutput, calls=%fused_computation.65 | convolution fusion | flops 1366030848 | bytes 17456640 | tf_op jit(solution)/shard_map/bctgxd,bcgde->bctgxe/dot_general | solution.py:89
  722.9 7.1 copy.61
  730.0 7.9 %reshape.309 = f32[4,384,768]{2,1,0:T(8,128)} reshape(f32[4,3,128,2,4,96]{5,4,3,2,1,0:T(4,128)} %copy.61) | data formatting | bytes 9437184 | tf_op jit(solution)/shard_map/reshape | solution.py:96
  737.9 15.0 %psum.7 = f32[4,384]{1,0:T(4,128)S(1)} all-reduce(f32[4,384]{1,0:T(4,128)S(1)} %bitcast.229), channel_id=1, replica_groups=mesh['ctx'=16,'head'=8] {'head'}, use_global_device_ids=true, to_apply=%region_13.14 | all-reduce | flops 1536 | bytes 12288 | tf_op jit(solution)/shard_map/psum | solution.py:156
  (340 shorter events, 452.3 us)
Async XLA Ops:
  6.5 66.2 %all-gather.7.cloned.1.call-start = ((), (), s32[]{:S(2)}) async-start(), calls=%async_computation.1 | async-start | bytes 3342336 | tf_op jit(solution)/shard_map/all_gather | solution.py:17
  14.6 4.4 copy-start.11
  18.0 4.2 copy-start.2
  19.0 4.0 copy-start.5
  22.3 173.5 %all-gather.5.cloned.1.call-start = ((), (), s32[]{:S(2)}) async-start(), calls=%async_computation | async-start | bytes 20054016 | tf_op jit(solution)/shard_map/all_gather | solution.py:98
  33.0 3.9 copy-start.10
  33.0 4.6 copy-start.3
  33.0 29.7 %copy-start.9 = (s32[4,3,16]{2,0,1:T(4,128)S(1)}, s32[4,3,16]{2,0,1:T(4,128)}, u32[]{:S(2)}) copy-start(s32[4,3,16]{2,0,1:T(4,128)} %param.11) | copy-start | bytes 2308
  37.0 54.9 %copy-start = (bf16[4,3,128,2,4,96]{2,5,4,3,1,0:T(8,128)(2,1)}, bf16[4,3,128,2,4,96]{2,5,4,3,1,0:T(8,128)(2,1)S(1)}, u32[]{:S(2)}) copy-start(bf16[4,3,128,2,4,96]{2,5,4,3,1,0:T(8,128)(2,1)S(1)} %fusion.42) | copy-start | bytes 7077892
  63.3 1.7 copy-start.6
  91.8 1.1 copy-start.8
  91.8 1.7 copy-start.4
  92.9 103.4 %copy-start.12 = (s32[4]{0:T(128)S(1)}, s32[4]{0:T(128)}, u32[]{:S(2)}) copy-start(s32[4]{0:T(128)} %param.12) | copy-start | bytes 52
  707.9 6.2 copy-start.1
  730.0 23.0 %copy-start.7 = (f32[768]{0:T(1024)S(1)}, f32[768]{0:T(1024)}, u32[]{:S(2)}) copy-start(f32[768]{0:T(1024)} %convert_element_type.87) | copy-start | bytes 9220
Sparse Core Ops, SparseCore 0:
  22.4 50.2 all-gather.6
  74.8 120.8 all-gather.4
where the time goes:
time: 771 us; the launch traced here: 766 us
  local copies, waits for them, and re-layouts  322 us (42%)
  matrix products  139 us (18%)
  other arithmetic  121 us (16%)
  waiting for transfers between devices  107 us (14%)
  blocking collectives  38.7 us (5%)
  loops' own time  23.4 us (3%)
  between operations  13.6 us (2%)
    gather x36, local copies, waits for them, and re-layouts, attend(): jnp.take(seq_pool, block_slots, axis=0).reshape(TOPK * BLK, kv_local, 2, HD)  180 us
    all_gather x1, waiting for transfers between devices, on_device(): candidates = lax.all_gather(kv_blocks, 'ctx', axis=1, tiled=True)  102 us
    sub x12, matrix products, attend(): weights = jnp.where(allowed[None, None], jnp.exp(scores - top_score), 0.0)  86.6 us
    squeeze x12, local copies, waits for them, and re-layouts, attend(): seq_pool = lax.dynamic_index_in_dim(candidates, seq_index, 0, False)  64 us
    dot_general x12, matrix products, attend(): jnp.einsum('ghxk,kge->xghe', weights.astype(jnp.bfloat16), picked[:, :, 1...  35.8 us
    select_n x24, other arithmetic, attend(): jnp.take(seq_pool, block_slots, axis=0).reshape(TOPK * BLK, kv_local, 2, HD)  26.6 us
    all_gather x1, blocking collectives, prefix(): lax.all_gather(part.astype(kind), axis)  23.7 us
    another operation x1, loops' own time, on_device(): lax.map(attend, jnp.arange(seq_count * stretch_count, dtype=jnp.int32))  22.9 us
  transfers between devices with their start and end apart: 2, of which 2 were waited for; matrix products, arithmetic and copies ran while one was open for 5% of the time, Pallas kernels for 0%

commit v1 on v0

--- a/solution.py
+++ b/solution.py
@@ -95,7 +95,9 @@
     )
     linear_out = linear_out.reshape(seq_count, local_len, feature_count)
     kv_blocks = keys_values.reshape(seq_count, stretch_count, BLK, kv_width)
-    candidates = lax.all_gather(kv_blocks, "ctx", axis=1, tiled=True)
+    candidates = jnp.concatenate(
+        lax.all_to_all(jnp.stack([kv_blocks] * lax.axis_size("ctx")), "ctx", 0, 0), axis=1
+    )
     slot_ids = jnp.maximum(block_lists, 0)
     offsets = jnp.arange(BLK, dtype=jnp.int32)
     score_scale = 1.0 / math.sqrt(HD)

time: 771 us -> 1010 us (1.31)
  blocking collectives: 38.7 us -> 357 us
  waiting for transfers between devices: 107 us -> 0.02 us
  local copies, waits for them, and re-layouts: 322 us -> 345 us
    all_gather x1, blocking collectives: 23.7 us -> 344 us  [prefix(): lax.all_gather(part.astype(kind), axis)]
    all_gather x1 -> x0, waiting for transfers between devices: 102 us -> none  [on_device(): candidates = lax.all_gather(kv_blocks, 'ctx', axis=1, tiled=True)]
    all_to_all x0 -> x1, local copies, waits for them, and re-layouts: none -> 18.9 us  [on_device(): lax.all_to_all(jnp.stack([kv_blocks] * lax.axis_size('ctx')), 'ctx', 0, 0)]
  transfers between devices with their start and end apart: 2 -> 2, of which waited for: 2 -> 0; matrix products, arithmetic and copies ran while one was open for 5% -> 5% of each run, Pallas kernels for 0% -> 0%
where the time goes in v1:
time: 1010 us
  blocking collectives  357 us (35%)
  local copies, waits for them, and re-layouts  345 us (34%)
  matrix products  139 us (14%)
  other arithmetic  121 us (12%)
  loops' own time  23.7 us (2%)
  between operations  13.7 us (1%)
    all_gather x1, blocking collectives, prefix(): lax.all_gather(part.astype(kind), axis)  344 us
    gather x36, local copies, waits for them, and re-layouts, attend(): jnp.take(seq_pool, block_slots, axis=0).reshape(TOPK * BLK, kv_local, 2, HD)  181 us
    sub x12, matrix products, attend(): weights = jnp.where(allowed[None, None], jnp.exp(scores - top_score), 0.0)  86.5 us
    squeeze x12, local copies, waits for them, and re-layouts, attend(): seq_pool = lax.dynamic_index_in_dim(candidates, seq_index, 0, False)  64 us
    dot_general x12, matrix products, attend(): jnp.einsum('ghxk,kge->xghe', weights.astype(jnp.bfloat16), picked[:, :, 1...  35.8 us
    select_n x24, other arithmetic, attend(): jnp.take(seq_pool, block_slots, axis=0).reshape(TOPK * BLK, kv_local, 2, HD)  26.9 us
    another operation x1, loops' own time, on_device(): lax.map(attend, jnp.arange(seq_count * stretch_count, dtype=jnp.int32))  23.2 us
    and x12, other arithmetic, attend(): listed[None, :] & (key_pos[None, :] <= query_pos[:, None])  20.8 us
  transfers between devices with their start and end apart: 2, of which 0 were waited for; matrix products, arithmetic and copies ran while one was open for 5% of the time, Pallas kernels for 0%

profile of v1, /device:TPU:0, one launch (start us, length us, event | category | flops | bytes accessed | tf_op | source)
XLA Modules:
  0.0 1007.1 jit_solution(7436414623634846141)
XLA Ops:
  6.5 8.2 stack.3
  14.7 7.3 all-to-all-start
  34.1 6.5 reshape.313
  49.3 344.0 %all-gather.1 = bf16[64,2,96]{2,1,0:T(2,128)(2,1)S(1)} all-gather(bf16[4,2,96]{2,1,0:T(2,128)(2,1)S(1)} %fusion.66), channel_id=3, replica_groups=mesh['ctx'=16,'head'=8] {'ctx'}, dimensions={0}, use_global_device_ids=true | all-gather | bytes 26112 | tf_op jit(solution)/shard_map/all_gather | solution.py:17
  399.3 18.9 %while.31 = (s32[]{:T(128)}, f32[4,2,96,96]{3,2,1,0:T(8,128)S(1)}, f32[4,2,96]{2,1,0:T(2,128)S(1)}, s32[]{:T(128)}, bf16[16,4,2,96,96]{4,3,2,1,0:T(8,128)(2,1)},...) while((s32[]{:T(128)}, f32[4,2,96,96]{3,2,1,0:T(8,128)S(1)}, ...), condition=%wide.region_3.4_spmd.clone, body=%wide.region_2.3_spmd.clone.sunk | while | flops 297988 | bytes 745083 | solution.py:34
  420.2 18.9 %copy.78 = bf16[16,4,3,128,384]{4,3,2,0,1:T(8,128)(2,1)} copy(bf16[16,4,3,128,384]{4,3,2,1,0:T(8,128)(2,1)} %all-to-all-done) | data formatting | bytes 37748736 | tf_op jit(solution)/shard_map/all_to_all | solution.py:99
  439.6 512.1 %while.30 = (s32[]{:T(128)}, f32[12,128,768]{1,2,0:T(8,128)}, s32[12]{0:T(128)}, s32[3,128]{1,0:T(4,128)S(1)}, s32[4]{0:T(128)S(1)}, /*index=5*/s32[4,3,16]{2,1,...) while((s32[]{:T(128)}, f32[12,128,768]{1,2,0:T(8,128)}, ...), condition=%wide.region_11.12_spmd.clone, body=%wide.region_8.11_spmd.clone.sunk | while | flops 819669376 | bytes 34196880 | solution.py:154
  471.3 7.2 fusion.98
  514.1 7.2 fusion.98
  556.8 7.2 fusion.98
  599.4 7.2 fusion.98
  642.0 7.2 fusion.98
  684.6 7.2 fusion.98
  727.3 7.2 fusion.98
  770.1 7.2 fusion.98
  799.6 6.3 reshape.350
  812.8 7.2 fusion.98
  855.5 7.2 fusion.98
  898.1 7.2 fusion.98
  940.8 7.2 fusion.98
  958.0 8.8 multiply_reduce_fusion
  966.8 7.1 copy.76
  973.9 7.9 reshape.314
  981.8 12.6 %psum.7 = f32[4,384]{1,0:T(4,128)S(1)} all-reduce(f32[4,384]{1,0:T(4,128)S(1)} %bitcast.233), channel_id=1, replica_groups=mesh['ctx'=16,'head'=8] {'head'}, use_global_device_ids=true, to_apply=%region_13.14 | all-reduce | flops 1536 | bytes 12288 | tf_op jit(solution)/shard_map/psum | solution.py:158
  (343 shorter events, 455.7 us)
Async XLA Ops:
  14.7 7.4 copy-start.4
  14.7 405.5 %all-to-all-start = ((bf16[16,4,3,128,384]{4,3,2,1,0:T(8,128)(2,1)}), bf16[16,4,3,128,384]{4,3,2,1,0:T(8,128)(2,1)}, u32[]{:S(2)}, u32[]{:S(2)}) async-start(bf16[16,4,3,128,384]{4,3,2,1,0:T(8,128)(2,1)} %stack.3), calls=%async_computation | async-start | bytes 37748736 | tf_op jit(solution)/shard_map/all_to_all | solution.py:99
  22.0 377.3 %all-gather.4.cloned.1.call-start = ((), (), s32[]{:S(2)}) async-start(), calls=%async_computation.1 | async-start | bytes 3342336 | tf_op jit(solution)/shard_map/all_gather | solution.py:17
  26.3 4.5 copy-start.12
  29.8 4.2 copy-start.2
  30.8 3.3 copy-start.6
  44.1 3.9 copy-start.11
  44.1 4.5 copy-start.3
  44.1 350.0 %copy-start.10 = (s32[4,3,16]{2,0,1:T(4,128)S(1)}, s32[4,3,16]{2,0,1:T(4,128)}, u32[]{:S(2)}) copy-start(s32[4,3,16]{2,0,1:T(4,128)} %param.11) | copy-start | bytes 2308
  48.0 370.3 %copy-start = (bf16[4,3,128,2,4,96]{2,5,4,3,1,0:T(8,128)(2,1)}, bf16[4,3,128,2,4,96]{2,5,4,3,1,0:T(8,128)(2,1)S(1)}, u32[]{:S(2)}) copy-start(bf16[4,3,128,2,4,96]{2,5,4,3,1,0:T(8,128)(2,1)S(1)} %fusion.42) | copy-start | bytes 7077892
  394.6 1.7 copy-start.7
  418.2 1.1 copy-start.9
  418.2 1.7 copy-start.5
  420.2 19.4 %copy-start.13 = (s32[4]{0:T(128)S(1)}, s32[4]{0:T(128)}, u32[]{:S(2)}) copy-start(s32[4]{0:T(128)} %param.12) | copy-start | bytes 52
  951.7 6.2 copy-start.1
  973.9 20.6 %copy-start.8 = (f32[768]{0:T(1024)S(1)}, f32[768]{0:T(1024)}, u32[]{:S(2)}) copy-start(f32[768]{0:T(1024)} %convert_element_type.87) | copy-start | bytes 9220
Sparse Core Ops, SparseCore 0:
  34.2 298.0 all-gather.3
